TPU v7x, 256 devices: a whole 4x4x8 slice. The times are simulated.
256 devices in a mesh: dp: 32 (over y, x, z_lo), mp: 8 (over z_hi, core).
Axes of the slice: x: 4, y: 4, z: 8 (z_hi: 4, z_lo: 2; z = z_hi * 2 + z_lo), core: 2. Of those that a mesh axis runs over, the one named last changes fastest.
Arguments:
- inputs: bfloat16 [4096, 16384], P('dp', 'mp'), may hold values from -6 to 6
- projector: bfloat16 [16384, 1024], P('dp', 'mp'), may hold values from -0.046875 to 0.046875
- out_grads: bfloat16 [4096, 26624], P('dp', 'mp'), may hold values from -0.25 to 0.25
- weights: bfloat16 [16384, 26624], P('dp', 'mp'), may hold values from -6 to 6
- first_moment: float32 [1024, 26624], P('dp', 'mp'), may hold values from -1.5 to 1.5
- second_moment: float32 [1024, 26624], P('dp', 'mp'), may hold values from 0.01 to 1
Outputs:
- new_weights: bfloat16 [16384, 26624], P('dp', 'mp')
- new_first: float32 [1024, 26624], P('dp', 'mp')
- new_second: float32 [1024, 26624], P('dp', 'mp')
All inputs are finite; a program needn't handle non-finite values.
Results may differ from a plain program's by a relative error of at most 0.0031.
Values may be sent and summed in bfloat16 or wider, within the bound.
A program may use at most 128 MiB of HBM per device.

v0:
```python
import jax
import jax.numpy as jnp
from jax import lax
from jax.sharding import Mesh
from jax.sharding import PartitionSpec as P

STEP = 1000
DP = ("dp_0", "dp_1", "dp_2")
MP = ("mp_0", "mp_1")


def joined_along(parts, dim):
    dims = list(parts.shape[1:])
    dims[dim] *= parts.shape[0]
    return jnp.moveaxis(parts, 0, dim).reshape(dims)


def copy_for_each(x, axis):
    peers = lax.axis_size(axis)
    return lax.all_to_all(jnp.broadcast_to(x[None], (peers, *x.shape)), axis, 0, 0, tiled=True)


def collect(x, axis, dim):
    return joined_along(copy_for_each(x, axis), dim)


def summed_rows(total, axes):
    for axis in axes:
        total = lax.psum_scatter(total, axis, scatter_dimension=0, tiled=True)
    return total


def stacked_from(x, axes, order):
    parts = x[None]
    for k in order:
        parts = lax.all_gather(parts, axes[k], axis=0, tiled=True)
    block = [lax.axis_size(axes[k]) for k in reversed(order)]
    parts = parts.reshape(*block, *x.shape)
    turned = sorted(range(len(order)), key=lambda place: order[len(order) - 1 - place])
    return parts.transpose(*turned, *range(len(order), parts.ndim)).reshape(-1, *x.shape)


def gather_axes(x, axes, order, dim):
    return joined_along(stacked_from(x, axes, order), dim)


def per_device(inputs, projector, out_grads, weights, first_moment, second_moment):
    columns = collect(projector, DP, 0)
    own_part = jnp.dot(
        lax.all_gather(inputs, MP, axis=1, tiled=True), columns, preferred_element_type=jnp.float32
    )
    projected = collect(own_part.astype(jnp.bfloat16), MP, 1)
    compressed = summed_rows(
        lax.dot_general(
            projected, out_grads, (((0,), (0,)), ((), ())), preferred_element_type=jnp.float32
        ),
        DP,
    )
    new_first = 0.9 * first_moment + 0.1 * compressed
    new_second = 0.999 * second_moment + 0.001 * compressed * compressed
    first_fix = 1.0 - 0.9**STEP
    second_fix = 1.0 - 0.999**STEP
    direction = (new_first / first_fix / (jnp.sqrt(new_second / second_fix) + 1e-08)).astype(
        jnp.bfloat16
    )
    full_rows = gather_axes(projector, MP, (0, 1), 1)
    empty = jnp.zeros(weights.shape, jnp.float32)
    piece = lax.all_gather(direction, DP, axis=0, tiled=True)
    ranks = lax.slice_in_dim(full_rows, 0, piece.shape[0], axis=1)
    lifted = empty + jnp.dot(ranks, piece, preferred_element_type=jnp.float32)
    new_weights = (weights.astype(jnp.float32) - 2.0 * lifted).astype(jnp.bfloat16)
    return (new_weights, new_first, new_second)


def solution(mesh):
    finer = Mesh(mesh.devices.reshape(4, 4, 2, 4, 2), ("dp_0", "dp_1", "dp_2", "mp_0", "mp_1"))
    in_specs = (P(DP, MP), P(DP, MP), P(DP, MP), P(DP, MP), P(DP, MP), P(DP, MP))
    out_specs = (P(DP, MP), P(DP, MP), P(DP, MP))
    return jax.shard_map(
        per_device, mesh=finer, in_specs=in_specs, out_specs=out_specs, check_vma=False
    )
```

profile of v0, /device:TPU:64, one launch (start us, length us, event | category | flops | bytes accessed | tf_op | source)
XLA Modules:
  0.0 534.7 jit_solution(4391776235239729843)
XLA Ops:
  8.0 0.0 copy-start
  8.0 3.9 broadcast_in_dim.6
  11.9 8.8 %all-to-all-start = ((bf16[32,512,128]{2,1,0:T(8,128)(2,1)}), bf16[32,512,128]{2,1,0:T(8,128)(2,1)}, u32[]{:S(2)}, u32[]{:S(2)}) async-start(bf16[32,512,128]{2,1,0:T(8,128)(2,1)} %broadcast_in_dim.6), calls=%async_computation | async-start | bytes 8388608 | tf_op jit(solution)/shard_map/all_to_all | solution.py:20
  20.7 0.0 all-gather.5.cloned.1.call-start
  20.8 0.7 all-gather.5.cloned.1.call-update
  21.5 0.0 reduce-scatter.4.cloned.1.call-start
  21.5 69.8 %all-gather.5.cloned.1.call-done = bf16[128,16384]{1,0:T(8,128)(2,1)} async-done(((bf16[128,2048]{1,0:T(8,128)(2,1)}), bf16[128,16384]{1,0:T(8,128)(2,1)}) %all-gather.5.cloned.1.call-update) | async-done | bytes 4194320 | tf_op jit(solution)/shard_map/all_gather | solution.py:50
  91.3 14.7 %all-to-all-done = bf16[32,512,128]{2,1,0:T(8,128)(2,1)} async-done(((bf16[32,512,128]{2,1,0:T(8,128)(2,1)}), bf16[32,512,128]{2,1,0:T(8,128)(2,1)}, u32[]{:S(2)}, u32[]{:S(2)}) %all-to-all-start) | async-done | bytes 4194336 | tf_op jit(solution)/shard_map/all_to_all | solution.py:20
  106.0 4.7 convolution_convert_fusion
  110.7 0.1 copy.21
  110.9 17.4 %all_to_all.10 = bf16[8,128,128]{1,2,0:T(8,128)(2,1)S(1)} all-to-all(bf16[8,128,128]{1,2,0:T(8,128)(2,1)S(1)} %broadcast_in_dim.7), channel_id=1, replica_groups=mesh['dp_0'=4,'dp_1'=4,'dp_2'=2,'mp_0'=4,'mp_1'=2] {'mp_0','mp_1'}, dimensions={0} | all-to-all | bytes 524288 | tf_op jit(solution)/shard_map/all_to_all | solution.py:20
  128.3 6.8 %fusion.3 = f32[1024,3328]{1,0:T(8,128)} fusion(bf16[128,1024]{0,1:T(8,128)(2,1)S(1)} %bitcast.24, bf16[128,3328]{1,0:T(8,128)(2,1)S(1)} %copy-done), kind=kOutput, calls=%fused_computation.7 | convolution fusion | flops 872415232 | bytes 14745600 | tf_op jit(solution)/shard_map/dot_general | solution.py:54
  135.1 0.0 reduce-scatter.4.cloned.1.call-update
  135.2 0.0 reduce-scatter.6.cloned.1.call-start
  135.2 119.8 %reduce-scatter.4.cloned.1.call-done = f32[256,3328]{1,0:T(8,128)} async-done(((f32[1024,3328]{1,0:T(8,128)}), f32[256,3328]{1,0:T(8,128)}) %reduce-scatter.4.cloned.1.call-update) | async-done | bytes 3407888 | tf_op jit(solution)/shard_map/reduce_scatter | solution.py:29
  255.0 0.0 reduce-scatter.6.cloned.1.call-update
  255.1 0.0 reduce-scatter.8.cloned.1.call-start
  255.1 45.2 %reduce-scatter.6.cloned.1.call-done = f32[64,3328]{1,0:T(8,128)} async-done(((f32[256,3328]{1,0:T(8,128)}), f32[64,3328]{1,0:T(8,128)}) %reduce-scatter.6.cloned.1.call-update) | async-done | bytes 851984 | tf_op jit(solution)/shard_map/reduce_scatter | solution.py:29
  300.3 0.0 reduce-scatter.8.cloned.1.call-update
  300.3 0.0 all-gather.9.cloned.1.call-start
  300.4 18.8 %all-gather = bf16[2048,128]{1,0:T(8,128)(2,1)} all-gather(bf16[512,128]{1,0:T(8,128)(2,1)S(1)} %copy-done.1), channel_id=2, replica_groups=mesh['dp_0'=4,'dp_1'=4,'dp_2'=2,'mp_0'=4,'mp_1'=2] {'mp_0'}, dimensions={0}, use_global_device_ids=true | all-gather | bytes 655360 | tf_op jit(solution)/shard_map/all_gather | solution.py:36
  319.2 0.0 all-gather.9.cloned.1.call-update
  319.2 0.0 all-gather.7.cloned.1.call-start
  319.3 8.0 %reduce-scatter.8.cloned.1.call-done = f32[32,3328]{1,0:T(8,128)} async-done(((f32[64,3328]{1,0:T(8,128)}), f32[32,3328]{1,0:T(8,128)}) %reduce-scatter.8.cloned.1.call-update) | async-done | bytes 426000 | tf_op jit(solution)/shard_map/reduce_scatter | solution.py:29
  327.3 2.1 divide_convert_fusion
  329.4 0.0 all-gather.7.cloned.1.call-update
  329.4 5.6 %copy.20 = bf16[512,3328]{0,1:T(8,128)(2,1)} copy(bf16[512,3328]{1,0:T(8,128)(2,1)} %param.9) | data formatting | bytes 6815744 | tf_op args[3]
  335.1 1.3 copy.22
  336.4 0.5 copy.23
  336.9 176.4 %all-gather.7.cloned.1.call-done = bf16[1024,3328]{1,0:T(8,128)(2,1)} async-done(((bf16[32,3328]{1,0:T(8,128)(2,1)}), bf16[1024,3328]{1,0:T(8,128)(2,1)}) %all-gather.7.cloned.1.call-update) | async-done | bytes 6815760 | tf_op jit(solution)/shard_map/all_gather | solution.py:68
  513.3 8.7 %fusion = bf16[512,3328]{0,1:T(8,128)(2,1)} fusion(bf16[512,3328]{0,1:T(8,128)(2,1)} %copy.20, bf16[1024,3328]{1,0:T(8,128)(2,1)} %all-gather.7.cloned.1.call-done, bf16[512,1024]{0,1:T(8,128)(2,1)S(1)} %bitcast.26), kind=kOutput, calls=%fused_computation.1 | convolution fusion | flops 3496476672 | bytes 14680064 | tf_op jit(solution)/shard_map/dot_general | solution.py:70
  522.0 5.5 %copy.24 = bf16[512,3328]{1,0:T(8,128)(2,1)} copy(bf16[512,3328]{0,1:T(8,128)(2,1)} %fusion) | data formatting | bytes 6815744
  (9 shorter events, 0.1 us)
Async XLA Ops:
  8.0 120.3 %copy-start = (bf16[128,3328]{1,0:T(8,128)(2,1)S(1)}, bf16[128,3328]{1,0:T(8,128)(2,1)}, u32[]{:S(2)}) copy-start(bf16[128,3328]{1,0:T(8,128)(2,1)} %param.8) | copy-start | bytes 2555908
  11.9 94.1 %all-to-all-start = ((bf16[32,512,128]{2,1,0:T(8,128)(2,1)}), bf16[32,512,128]{2,1,0:T(8,128)(2,1)}, u32[]{:S(2)}, u32[]{:S(2)}) async-start(bf16[32,512,128]{2,1,0:T(8,128)(2,1)} %broadcast_in_dim.6), calls=%async_computation | async-start | bytes 8388608 | tf_op jit(solution)/shard_map/all_to_all | solution.py:20
  20.7 70.6 %all-gather.5.cloned.1.call-start = ((), (), s32[]{:S(2)}) async-start(), calls=%async_computation.5 | async-start | bytes 4718592 | tf_op jit(solution)/shard_map/all_gather | solution.py:50
  21.5 233.6 %reduce-scatter.4.cloned.1.call-start = ((), (), s32[]{:S(2)}) async-start(), calls=%async_computation.6 | async-start | bytes 17039360 | tf_op jit(solution)/shard_map/reduce_scatter | solution.py:29
  135.1 165.3 %copy-start.1 = (bf16[512,128]{1,0:T(8,128)(2,1)S(1)}, bf16[512,128]{1,0:T(8,128)(2,1)}, u32[]{:S(2)}) copy-start(bf16[512,128]{1,0:T(8,128)(2,1)} %param.7) | copy-start | bytes 393220
  135.2 192.2 %copy-start.2 = (f32[32,3328]{1,0:T(8,128)S(1)}, f32[32,3328]{1,0:T(8,128)}, u32[]{:S(2)}) copy-start(f32[32,3328]{1,0:T(8,128)} %param.11) | copy-start | bytes 1277956
  135.2 192.1 %copy-start.3 = (f32[32,3328]{1,0:T(8,128)S(1)}, f32[32,3328]{1,0:T(8,128)}, u32[]{:S(2)}) copy-start(f32[32,3328]{1,0:T(8,128)} %param.10) | copy-start | bytes 1277956
  135.2 165.1 %reduce-scatter.6.cloned.1.call-start = ((), (), s32[]{:S(2)}) async-start(), calls=%async_computation.7 | async-start | bytes 4259840 | tf_op jit(solution)/shard_map/reduce_scatter | solution.py:29
  255.1 72.2 %reduce-scatter.8.cloned.1.call-start = ((), (), s32[]{:S(2)}) async-start(), calls=%async_computation.8 | async-start | bytes 1277952 | tf_op jit(solution)/shard_map/reduce_scatter | solution.py:29
  300.3 34.7 %all-gather.9.cloned.1.call-start = ((), (), s32[]{:S(2)}) async-start(), calls=%async_computation.10 | async-start | bytes 1572864 | tf_op jit(solution)/shard_map/all_gather | solution.py:36
  319.2 194.1 %all-gather.7.cloned.1.call-start = ((), (), s32[]{:S(2)}) async-start(), calls=%async_computation.9 | async-start | bytes 7028736 | tf_op jit(solution)/shard_map/all_gather | solution.py:68
Sparse Core Ops, SparseCore 0:
  23.4 67.9 all-gather.4
  135.3 119.7 reduce-scatter.3
  257.6 42.6 reduce-scatter.5
  302.7 24.5 reduce-scatter.7
Sparse Core Ops, SparseCore 1:
  319.3 13.1 all-gather.8
  334.1 179.2 all-gather.6
where the time goes:
time: 535 us
  waiting for transfers between devices  435 us (81%)
  blocking collectives  36.1 us (7%)
  matrix products  20.3 us (4%)
  local copies, waits for them, and re-layouts  17.1 us (3%)
  between operations  15.3 us (3%)
  starting transfers between devices  9.05 us (2%)
    all_gather x1, waiting for transfers between devices, per_device(): piece = lax.all_gather(direction, DP, axis=0, tiled=True)  176 us
    reduce_scatter x3, waiting for transfers between devices, summed_rows(): total = lax.psum_scatter(total, axis, scatter_dimension=0, tiled=True)  173 us
    all_gather x1, waiting for transfers between devices, per_device(): lax.all_gather(inputs, MP, axis=1, tiled=True)  69.8 us
    all_gather x1, blocking collectives, stacked_from(): parts = lax.all_gather(parts, axes[k], axis=0, tiled=True)  18.8 us
    all_to_all x1, blocking collectives, copy_for_each(): lax.all_to_all(jnp.broadcast_to(x[None], (peers, *x.shape)), axis, 0, 0,...  17.4 us
    all_to_all x1, waiting for transfers between devices, copy_for_each(): lax.all_to_all(jnp.broadcast_to(x[None], (peers, *x.shape)), axis, 0, 0,...  14.7 us
    unnamed x10, local copies, waits for them, and re-layouts  11.2 us
  transfers between devices with their start and end apart: 7, of which 6 were waited for; matrix products, arithmetic and copies ran while one was open for 2% of the time, Pallas kernels for 0%

commit v1 on v0

--- a/solution.py
+++ b/solution.py
@@ -65,7 +65,9 @@
     )
     full_rows = gather_axes(projector, MP, (0, 1), 1)
     empty = jnp.zeros(weights.shape, jnp.float32)
-    piece = lax.all_gather(direction, DP, axis=0, tiled=True)
+    piece = jnp.concatenate(
+        lax.all_to_all(jnp.stack([direction] * lax.axis_size(DP)), DP, 0, 0), axis=0
+    )
     ranks = lax.slice_in_dim(full_rows, 0, piece.shape[0], axis=1)
     lifted = empty + jnp.dot(ranks, piece, preferred_element_type=jnp.float32)
     new_weights = (weights.astype(jnp.float32) - 2.0 * lifted).astype(jnp.bfloat16)

time: 535 us -> 497 us (0.929)
  waiting for transfers between devices: 435 us -> 293 us
  blocking collectives: 36.1 us -> 126 us
  starting transfers between devices: 9.05 us -> 16.3 us
    all_gather x1 -> x0, waiting for transfers between devices: 176 us -> none  [per_device(): piece = lax.all_gather(direction, DP, axis=0, tiled=True)]
    all_gather x1, blocking collectives: 18.8 us -> 109 us  [stacked_from(): parts = lax.all_gather(parts, axes[k], axis=0, tiled=True)]
    reduce_scatter x3, waiting for transfers between devices: 173 us -> 191 us  [summed_rows(): total = lax.psum_scatter(total, axis, scatter_dimension=0, tiled=True)]
    all_gather x1, waiting for transfers between devices: 0.01 us -> 17.4 us  [stacked_from(): parts = lax.all_gather(parts, axes[k], axis=0, tiled=True)]
    all_to_all x0 -> x1, starting transfers between devices: none -> 7.34 us  [per_device(): lax.all_to_all(jnp.stack([direction] * lax.axis_size(DP)), DP, 0, 0)]
  transfers between devices with their start and end apart: 7 -> 7, of which waited for: 6 -> 6; matrix products, arithmetic and copies ran while one was open for 2% -> 1% of each run, Pallas kernels for 0% -> 0%
where the time goes in v1:
time: 497 us; the launch traced here: 494 us
  waiting for transfers between devices  293 us (59%)
  blocking collectives  126 us (25%)
  local copies, waits for them, and re-layouts  20.6 us (4%)
  matrix products  20.3 us (4%)
  starting transfers between devices  16.3 us (3%)
  between operations  15.3 us (3%)
    reduce_scatter x3, waiting for transfers between devices, summed_rows(): total = lax.psum_scatter(total, axis, scatter_dimension=0, tiled=True)  191 us
    all_gather x1, blocking collectives, stacked_from(): parts = lax.all_gather(parts, axes[k], axis=0, tiled=True)  109 us
    all_gather x1, waiting for transfers between devices, per_device(): lax.all_gather(inputs, MP, axis=1, tiled=True)  69.8 us
    all_gather x1, waiting for transfers between devices, stacked_from(): parts = lax.all_gather(parts, axes[k], axis=0, tiled=True)  17.4 us
    all_to_all x1, blocking collectives, copy_for_each(): lax.all_to_all(jnp.broadcast_to(x[None], (peers, *x.shape)), axis, 0, 0,...  17.4 us
    all_to_all x1, waiting for transfers between devices, copy_for_each(): lax.all_to_all(jnp.broadcast_to(x[None], (peers, *x.shape)), axis, 0, 0,...  14.7 us
    unnamed x10, local copies, waits for them, and re-layouts  11.1 us
  transfers between devices with their start and end apart: 7, of which 6 were waited for; matrix products, arithmetic and copies ran while one was open for 1% of the time, Pallas kernels for 0%

profile of v1, /device:TPU:64, one launch (start us, length us, event | category | flops | bytes accessed | tf_op | source)
XLA Modules:
  0.0 494.2 jit_solution(10229775811812718573)
XLA Ops:
  8.0 0.0 copy-start
  8.0 3.9 broadcast_in_dim.6
  11.9 8.8 %all-to-all-start = ((bf16[32,512,128]{2,1,0:T(8,128)(2,1)}), bf16[32,512,128]{2,1,0:T(8,128)(2,1)}, u32[]{:S(2)}, u32[]{:S(2)}) async-start(bf16[32,512,128]{2,1,0:T(8,128)(2,1)} %broadcast_in_dim.6), calls=%async_computation | async-start | bytes 8388608 | tf_op jit(solution)/shard_map/all_to_all | solution.py:20
  20.7 0.0 all-gather.4.cloned.1.call-start
  20.8 0.7 all-gather.4.cloned.1.call-update
  21.4 0.0 reduce-scatter.4.cloned.1.call-start
  21.5 69.8 %all-gather.4.cloned.1.call-done = bf16[128,16384]{1,0:T(8,128)(2,1)} async-done(((bf16[128,2048]{1,0:T(8,128)(2,1)}), bf16[128,16384]{1,0:T(8,128)(2,1)}) %all-gather.4.cloned.1.call-update) | async-done | bytes 4194320 | tf_op jit(solution)/shard_map/all_gather | solution.py:50
  91.3 14.7 %all-to-all-done = bf16[32,512,128]{2,1,0:T(8,128)(2,1)} async-done(((bf16[32,512,128]{2,1,0:T(8,128)(2,1)}), bf16[32,512,128]{2,1,0:T(8,128)(2,1)}, u32[]{:S(2)}, u32[]{:S(2)}) %all-to-all-start) | async-done | bytes 4194336 | tf_op jit(solution)/shard_map/all_to_all | solution.py:20
  106.0 4.7 convolution_convert_fusion
  110.7 0.1 copy.21
  110.9 17.4 %all_to_all.15 = bf16[8,128,128]{1,2,0:T(8,128)(2,1)S(1)} all-to-all(bf16[8,128,128]{1,2,0:T(8,128)(2,1)S(1)} %broadcast_in_dim.7), channel_id=1, replica_groups=mesh['dp_0'=4,'dp_1'=4,'dp_2'=2,'mp_0'=4,'mp_1'=2] {'mp_0','mp_1'}, dimensions={0} | all-to-all | bytes 524288 | tf_op jit(solution)/shard_map/all_to_all | solution.py:20
  128.3 6.8 %fusion.3 = f32[1024,3328]{1,0:T(8,128)} fusion(bf16[128,1024]{0,1:T(8,128)(2,1)S(1)} %bitcast.25, bf16[128,3328]{1,0:T(8,128)(2,1)S(1)} %copy-done), kind=kOutput, calls=%fused_computation.7 | convolution fusion | flops 872415232 | bytes 14745600 | tf_op jit(solution)/shard_map/dot_general | solution.py:54
  135.1 0.0 reduce-scatter.4.cloned.1.call-update
  135.2 0.0 reduce-scatter.6.cloned.1.call-start
  135.2 119.8 %reduce-scatter.4.cloned.1.call-done = f32[256,3328]{1,0:T(8,128)} async-done(((f32[1024,3328]{1,0:T(8,128)}), f32[256,3328]{1,0:T(8,128)}) %reduce-scatter.4.cloned.1.call-update) | async-done | bytes 3407888 | tf_op jit(solution)/shard_map/reduce_scatter | solution.py:29
  255.0 0.0 reduce-scatter.6.cloned.1.call-update
  255.1 0.0 reduce-scatter.8.cloned.1.call-start
  255.1 45.2 %reduce-scatter.6.cloned.1.call-done = f32[64,3328]{1,0:T(8,128)} async-done(((f32[256,3328]{1,0:T(8,128)}), f32[64,3328]{1,0:T(8,128)}) %reduce-scatter.6.cloned.1.call-update) | async-done | bytes 851984 | tf_op jit(solution)/shard_map/reduce_scatter | solution.py:29
  300.3 0.0 reduce-scatter.8.cloned.1.call-update
  300.3 25.6 %reduce-scatter.8.cloned.1.call-done = f32[32,3328]{1,0:T(8,128)} async-done(((f32[64,3328]{1,0:T(8,128)}), f32[32,3328]{1,0:T(8,128)}) %reduce-scatter.8.cloned.1.call-update) | async-done | bytes 426000 | tf_op jit(solution)/shard_map/reduce_scatter | solution.py:29
  325.9 2.2 divide_convert_fusion
  328.1 3.7 stack.2
  331.7 7.3 %all-to-all-start.2 = ((bf16[32,32,3328]{2,1,0:T(8,128)(2,1)}), bf16[32,32,3328]{2,1,0:T(8,128)(2,1)}, u32[]{:S(2)}, u32[]{:S(2)}) async-start(bf16[32,32,3328]{2,1,0:T(8,128)(2,1)} %stack.2), calls=%async_computation.5 | async-start | bytes 13631488 | tf_op jit(solution)/shard_map/all_to_all | solution.py:69
  339.1 0.0 all-gather.6.cloned.1.call-start
  339.1 108.9 %all-gather = bf16[2048,128]{1,0:T(8,128)(2,1)} all-gather(bf16[512,128]{1,0:T(8,128)(2,1)S(1)} %copy-done.1), channel_id=2, replica_groups=mesh['dp_0'=4,'dp_1'=4,'dp_2'=2,'mp_0'=4,'mp_1'=2] {'mp_0'}, dimensions={0}, use_global_device_ids=true | all-gather | bytes 655360 | tf_op jit(solution)/shard_map/all_gather | solution.py:36
  448.0 0.0 all-gather.6.cloned.1.call-update
  448.0 5.6 %copy.20 = bf16[512,3328]{0,1:T(8,128)(2,1)} copy(bf16[512,3328]{1,0:T(8,128)(2,1)} %param.9) | data formatting | bytes 6815744 | tf_op args[3]
  453.6 17.4 %all-gather.6.cloned.1.call-done = bf16[8,512,128]{2,1,0:T(8,128)(2,1)} async-done(((bf16[4,512,128]{2,1,0:T(8,128)(2,1)}), bf16[8,512,128]{2,1,0:T(8,128)(2,1)}) %all-gather.6.cloned.1.call-update) | async-done | bytes 1048592 | tf_op jit(solution)/shard_map/all_gather | solution.py:36
  471.0 1.3 copy.22
  472.3 0.5 copy.23
  472.8 8.8 %fusion = bf16[512,3328]{0,1:T(8,128)(2,1)} fusion(bf16[512,3328]{0,1:T(8,128)(2,1)} %copy.20, bf16[1024,3328]{1,0:T(8,128)(2,1)} %bitcast.3, bf16[512,1024]{0,1:T(8,128)(2,1)S(1)} %bitcast.27), kind=kOutput, calls=%fused_computation.1 | convolution fusion | flops 3496476672 | bytes 14680064 | tf_op jit(solution)/shard_map/dot_general | solution.py:72
  481.6 5.5 %copy.24 = bf16[512,3328]{1,0:T(8,128)(2,1)} copy(bf16[512,3328]{0,1:T(8,128)(2,1)} %fusion) | data formatting | bytes 6815744
  (9 shorter events, 0.1 us)
Async XLA Ops:
  8.0 120.3 %copy-start = (bf16[128,3328]{1,0:T(8,128)(2,1)S(1)}, bf16[128,3328]{1,0:T(8,128)(2,1)}, u32[]{:S(2)}) copy-start(bf16[128,3328]{1,0:T(8,128)(2,1)} %param.8) | copy-start | bytes 2555908
  11.9 94.1 %all-to-all-start = ((bf16[32,512,128]{2,1,0:T(8,128)(2,1)}), bf16[32,512,128]{2,1,0:T(8,128)(2,1)}, u32[]{:S(2)}, u32[]{:S(2)}) async-start(bf16[32,512,128]{2,1,0:T(8,128)(2,1)} %broadcast_in_dim.6), calls=%async_computation | async-start | bytes 8388608 | tf_op jit(solution)/shard_map/all_to_all | solution.py:20
  20.7 70.6 %all-gather.4.cloned.1.call-start = ((), (), s32[]{:S(2)}) async-start(), calls=%async_computation.6 | async-start | bytes 4718592 | tf_op jit(solution)/shard_map/all_gather | solution.py:50
  21.4 233.6 %reduce-scatter.4.cloned.1.call-start = ((), (), s32[]{:S(2)}) async-start(), calls=%async_computation.7 | async-start | bytes 17039360 | tf_op jit(solution)/shard_map/reduce_scatter | solution.py:29
  135.1 190.8 %copy-start.2 = (f32[32,3328]{1,0:T(8,128)S(1)}, f32[32,3328]{1,0:T(8,128)}, u32[]{:S(2)}) copy-start(f32[32,3328]{1,0:T(8,128)} %param.11) | copy-start | bytes 1277956
  135.1 190.8 %copy-start.3 = (f32[32,3328]{1,0:T(8,128)S(1)}, f32[32,3328]{1,0:T(8,128)}, u32[]{:S(2)}) copy-start(f32[32,3328]{1,0:T(8,128)} %param.10) | copy-start | bytes 1277956
  135.2 165.2 %reduce-scatter.6.cloned.1.call-start = ((), (), s32[]{:S(2)}) async-start(), calls=%async_computation.8 | async-start | bytes 4259840 | tf_op jit(solution)/shard_map/reduce_scatter | solution.py:29
  255.1 70.8 %reduce-scatter.8.cloned.1.call-start = ((), (), s32[]{:S(2)}) async-start(), calls=%async_computation.9 | async-start | bytes 1277952 | tf_op jit(solution)/shard_map/reduce_scatter | solution.py:29
  331.7 7.4 %copy-start.1 = (bf16[512,128]{1,0:T(8,128)(2,1)S(1)}, bf16[512,128]{1,0:T(8,128)(2,1)}, u32[]{:S(2)}) copy-start(bf16[512,128]{1,0:T(8,128)(2,1)} %param.7) | copy-start | bytes 393220
  331.7 141.1 %all-to-all-start.2 = ((bf16[32,32,3328]{2,1,0:T(8,128)(2,1)}), bf16[32,32,3328]{2,1,0:T(8,128)(2,1)}, u32[]{:S(2)}, u32[]{:S(2)}) async-start(bf16[32,32,3328]{2,1,0:T(8,128)(2,1)} %stack.2), calls=%async_computation.5 | async-start | bytes 13631488 | tf_op jit(solution)/shard_map/all_to_all | solution.py:69
  339.1 131.9 %all-gather.6.cloned.1.call-start = ((), (), s32[]{:S(2)}) async-start(), calls=%async_computation.10 | async-start | bytes 1572864 | tf_op jit(solution)/shard_map/all_gather | solution.py:36
Sparse Core Ops, SparseCore 0:
  23.4 67.9 all-gather.3
  135.3 119.7 reduce-scatter.3
  257.6 42.6 reduce-scatter.5
  302.7 23.1 reduce-scatter.7
Sparse Core Ops, SparseCore 1:
  448.1 22.8 all-gather.5
